TPU v7x, 256 devices: a whole 4x4x8 slice. The times are simulated.
256 devices in a mesh: head: 8 (over y, core), doc: 32 (over x, z).
Axes of the slice: x: 4, y: 4, z: 8, core: 2. Of those that a mesh axis runs over, the one named last changes fastest.
Arguments:
- tokens: bfloat16 [12288, 1024], P('doc'), may hold values from -6 to 6
- w_qkv: bfloat16 [1024, 3, 1024], P(None, None, 'head'), may hold values from -0.1875 to 0.1875
- w_out: bfloat16 [1024, 1024], P('head'), may hold values from -0.1875 to 0.1875
- w_up: bfloat16 [1024, 4096], P(None, 'head'), may hold values from -0.1875 to 0.1875
- w_down: bfloat16 [4096, 1024], P('head'), may hold values from -0.09375 to 0.09375
- gain_one: float32 [1024], replicated, may hold values from 0.5 to 1.5
- gain_two: float32 [1024], replicated, may hold values from 0.5 to 1.5
- rel_table: bfloat16 [512, 1024], replicated, may hold values from -6 to 6
- prompt_cache: bfloat16 [2, 4096, 1024], P(None, 'doc', 'head'), may hold values from -480 to 480
- w_proj: bfloat16 [1024, 128], replicated, may hold values from -0.1875 to 0.1875
- doc_vectors: bfloat16 [2048, 256, 128], P('doc'), may hold values from -0.5 to 0.5
- doc_lengths: int32 [2048], P('doc'), may hold values from 8 to 256, as said below
- group_ids: int32 [384], P('doc'), may hold values from 0 to 63
- candidates: int32 [384, 64], P('doc', 'head'), may hold values from 0 to 2047, as said below
Outputs:
- query_vectors: bfloat16 [12288, 128], P('doc')
- scores: float32 [384, 64], P('doc', 'head')
Inputs may be any that keep to these rules, and one draw needn't show every extreme that they name: Split candidates into aligned blocks of 12 requests by 8 columns (one index of doc with one of head). Index o of doc holds documents o * 64 to o * 64 + 63. In each block at most 6 entries name documents held by one index of doc, and one index of doc, the same for all blocks, is named by exactly 6 entries of every block. The documents named within one block are distinct. Some document has exactly 256 tokens; token slots from doc_lengths on are padding.
All inputs are finite; a program needn't handle non-finite values.
Results may differ from a plain program's by a relative error of at most 0.02.
Values may be sent and summed in bfloat16 or wider, within the bound.
A program may use at most 128 MiB of HBM per device.

v0:
```python
import math
import jax
import jax.numpy as jnp
from jax import lax
from jax.sharding import PartitionSpec as P

HD = 64
RELS = 512
QLEN = 32
PLEN = 64
DOC_DEV = 64


def layer_norm(values, gain):
    centre = values - jnp.mean(values, axis=-1, keepdims=True)
    spread = jnp.mean(centre * centre, axis=-1, keepdims=True)
    return centre * lax.rsqrt(spread + 1e-07) * gain


def slot_order(holders):
    count = holders.shape[0]
    same = holders[:, None] == holders[None, :]
    earlier = jnp.arange(count)[:, None] > jnp.arange(count)[None, :]
    return jnp.sum(same & earlier, axis=1)


def rate_slots(slot_query, slot_doc, doc_vectors, doc_lengths):
    shape = slot_doc.shape
    flat_doc = slot_doc.reshape(-1)
    flat_query = slot_query.reshape((flat_doc.shape[0],) + slot_query.shape[-2:])
    safe_doc = jnp.maximum(flat_doc, 0)
    documents = doc_vectors[safe_doc]
    lengths = doc_lengths[safe_doc]
    sims = jnp.einsum("sqe,sje->sqj", flat_query, documents, preferred_element_type=jnp.float32)
    live = jnp.arange(documents.shape[1], dtype=jnp.int32)[None, None, :] < lengths[:, None, None]
    best = jnp.max(jnp.where(live, sims, -jnp.inf), axis=2)
    totals = jnp.where(flat_doc >= 0, jnp.sum(best, axis=1), 0.0)
    return totals.reshape(shape)


def body(
    tokens,
    w_qkv,
    w_out,
    w_up,
    w_down,
    gain_one,
    gain_two,
    rel_table,
    prompt_cache,
    w_proj,
    doc_vectors,
    doc_lengths,
    group_ids,
    candidates,
):
    rows_dev = tokens.shape[0]
    req_dev = rows_dev // QLEN
    width = w_qkv.shape[2]
    heads_loc = width // HD
    half = RELS // 2
    scale_root = math.sqrt(3 * HD)
    gathered = lax.all_gather(prompt_cache, "doc", axis=1, tiled=True)
    weights_split = w_qkv.reshape(w_qkv.shape[0], 3, heads_loc, HD)
    projected_all = jnp.einsum(
        "td,dchf->chtf", tokens, weights_split, preferred_element_type=jnp.float32
    ).astype(jnp.bfloat16)
    rel_both = jnp.einsum(
        "rd,dchf->chrf", rel_table, weights_split[:, :2], preferred_element_type=jnp.float32
    ).astype(jnp.bfloat16)
    head_shape = (heads_loc, req_dev, QLEN, HD)
    query_four = projected_all[0].reshape(head_shape)
    keys_four = projected_all[1].reshape(head_shape)
    values_four = projected_all[2].reshape(head_shape)
    groups_all = gathered.shape[1] // PLEN
    cache_all = gathered.reshape(2, groups_all, PLEN, heads_loc, HD)
    picked = jnp.transpose(cache_all[:, group_ids], (0, 3, 1, 2, 4))
    keys = jnp.concatenate([keys_four, picked[0]], axis=2)
    values = jnp.concatenate([values_four, picked[1]], axis=2)
    pos_query = PLEN + jnp.arange(QLEN, dtype=jnp.int32)
    pos_key = jnp.concatenate([pos_query, jnp.arange(PLEN, dtype=jnp.int32)])
    index_one = pos_query[:, None] - pos_key[None, :] + half
    index_two = pos_key[:, None] - pos_query[None, :] + half
    rel_k_rows = rel_both[1][:, index_one]
    rel_q_rows = rel_both[0][:, index_two]
    c2p = jnp.einsum("hrqd,hqkd->hrqk", query_four, rel_k_rows, preferred_element_type=jnp.float32)
    p2c = jnp.einsum("hrkd,hkqd->hrqk", keys, rel_q_rows, preferred_element_type=jnp.float32)
    content = jnp.einsum("hrqd,hrkd->hrqk", query_four, keys, preferred_element_type=jnp.float32)
    logits = (content + c2p + p2c) / scale_root
    largest = jnp.max(logits, axis=-1, keepdims=True)
    weights = jnp.exp(logits - largest)
    denominator = jnp.sum(weights, axis=-1)
    summed = jnp.einsum(
        "hrqk,hrkd->hrqd", weights.astype(jnp.bfloat16), values, preferred_element_type=jnp.float32
    )
    attended = (summed / denominator[..., None]).astype(jnp.bfloat16)
    out_split = w_out.reshape(heads_loc, HD, w_out.shape[1])
    attn_part = jnp.einsum(
        "hrqd,hde->rqe", attended, out_split, preferred_element_type=jnp.float32
    ).reshape(rows_dev, w_out.shape[1])
    attn_total = lax.psum(attn_part.astype(jnp.bfloat16), "head").astype(jnp.float32)
    hidden_one = layer_norm(tokens.astype(jnp.float32) + attn_total, gain_one).astype(jnp.bfloat16)
    inner = jax.nn.gelu(
        jnp.dot(hidden_one, w_up, preferred_element_type=jnp.float32), approximate=False
    ).astype(jnp.bfloat16)
    ffn_total = lax.psum(
        jnp.dot(inner, w_down, preferred_element_type=jnp.float32).astype(jnp.bfloat16), "head"
    ).astype(jnp.float32)
    hidden_two = layer_norm(hidden_one.astype(jnp.float32) + ffn_total, gain_two).astype(
        jnp.bfloat16
    )
    projected = jnp.dot(hidden_two, w_proj, preferred_element_type=jnp.float32)
    query_vectors = (
        projected * lax.rsqrt(jnp.sum(projected * projected, axis=-1, keepdims=True) + 1e-06)
    ).astype(jnp.bfloat16)
    shards = lax.axis_size("doc")
    cand_dev = candidates.shape[1]
    pairs = req_dev * cand_dev
    capacity = max(2, 2 * pairs // shards)
    flat_cand = candidates.reshape(-1)
    holders = flat_cand // DOC_DEV
    request_of = jnp.arange(pairs, dtype=jnp.int32) // cand_dev
    slot_rank = slot_order(holders)
    copies, cand_copies = (
        lax.all_gather(query_vectors, "doc", axis=0, tiled=True),
        lax.all_gather(candidates, "doc", axis=0, tiled=True),
    )
    all_query = copies.reshape(shards, req_dev, QLEN, copies.shape[1])
    all_cand = cand_copies.reshape(shards, pairs)
    holder_all = all_cand // DOC_DEV
    local_all = all_cand % DOC_DEV
    rank_all = jax.vmap(slot_order)(holder_all)
    own_index = lax.axis_index("doc")
    chosen = (holder_all[:, None, :] == own_index) & (
        rank_all[:, None, :] == jnp.arange(capacity, dtype=jnp.int32)[None, :, None]
    )
    filled = jnp.any(chosen, axis=2)
    slot_request = jnp.sum(jnp.where(chosen, request_of[None, None, :], 0), axis=2)
    slot_doc = jnp.where(
        filled, jnp.sum(jnp.where(chosen, local_all[:, None, :], 0), axis=2), -1
    ).astype(jnp.int32)
    slot_query = all_query[jnp.arange(shards)[:, None], slot_request]
    slot_scores = rate_slots(slot_query, slot_doc, doc_vectors, doc_lengths)
    returned = lax.all_to_all(slot_scores, "doc", split_axis=0, concat_axis=0, tiled=True)
    scores = returned.reshape(-1)[holders * capacity + slot_rank].reshape(candidates.shape)
    return (query_vectors, scores)


def solution(mesh):
    placed = (
        P("doc", None),
        P(None, None, "head"),
        P("head", None),
        P(None, "head"),
        P("head", None),
        P(),
        P(),
        P(),
        P(None, "doc", "head"),
        P(),
        P("doc", None, None),
        P("doc"),
        P("doc"),
        P("doc", "head"),
    )
    return jax.shard_map(
        body,
        mesh=mesh,
        in_specs=placed,
        out_specs=(P("doc", None), P("doc", "head")),
        check_vma=False,
    )
```

profile of v0, /device:TPU:8, one launch (start us, length us, event | category | flops | bytes accessed | tf_op | source)
XLA Modules:
  0.0 386.3 jit_solution(13940295378734445451)
XLA Ops:
  7.2 0.7 all-gather.4.cloned.1.call-update
  8.2 1.4 copy.182
  9.7 0.5 fusion.9
  10.4 20.3 %gather_fusion.2 = bf16[3072,2,64]{2,1,0:T(2,128)(2,1)} fusion(bf16[2,512,64]{2,0,1:T(2,128)(2,1)S(1)} %copy.193, s32[3072]{0:T(1024)S(1)} %broadcast_clamp_fusion), kind=kCustom, calls=%fused_computation.2 | custom fusion | bytes 1585152 | tf_op jit(solution)/shard_map/gather | solution.py:85
  30.6 2.9 copy.194
  33.6 0.6 fusion.8
  34.1 0.7 fusion.103
  35.6 20.3 %gather_fusion.1 = bf16[3072,2,64]{2,1,0:T(2,128)(2,1)} fusion(bf16[2,512,64]{2,0,1:T(2,128)(2,1)S(1)} %copy.189, s32[3072]{0:T(1024)S(1)} %broadcast_clamp_fusion.1), kind=kCustom, calls=%fused_computation.1 | custom fusion | bytes 1585152 | tf_op jit(solution)/shard_map/gather | solution.py:84
  55.9 4.0 %copy.190 = bf16[32,96,2,64]{1,3,0,2:T(8,128)(2,1)S(1)} copy(bf16[32,96,2,64]{3,2,1,0:T(2,128)(2,1)} %bitcast.83) | data formatting | bytes 1572864 | tf_op jit(solution)/shard_map/gather | solution.py:84
  59.9 1.1 copy.183
  61.0 1.7 copy.197
  62.7 1.9 copy.198
  64.6 1.2 fusion.11
  65.7 25.8 %all-gather.4.cloned.1.call-done = bf16[2,4096,128]{2,1,0:T(8,128)(2,1)} async-done(((bf16[2,128,128]{2,1,0:T(8,128)(2,1)}), bf16[2,4096,128]{2,1,0:T(8,128)(2,1)}) %all-gather.4.cloned.1.call-update) | async-done | bytes 2097168 | tf_op jit(solution)/shard_map/all_gather | solution.py:63
  91.5 8.2 %reshape.599 = bf16[2,64,64,2,64]{4,3,2,1,0:T(2,128)(2,1)} reshape(bf16[2,4096,128]{2,1,0:T(8,128)(2,1)} %all-gather.4.cloned.1.call-done) | data formatting | bytes 4194304 | tf_op jit(solution)/shard_map/reshape | solution.py:76
  99.7 5.4 %copy.186 = bf16[2,64,64,2,64]{4,2,3,1,0:T(8,128)(2,1)} copy(bf16[2,64,64,2,64]{4,3,2,1,0:T(2,128)(2,1)} %reshape.599) | data formatting | bytes 4194304 | tf_op jit(solution)/shard_map/reshape | solution.py:76
  105.2 3.7 gather_fusion
  108.9 1.5 copy.187
  110.4 0.8 slice_bitcast_fusion.1
  111.4 0.6 copy.195
  112.1 3.5 fusion.107
  115.6 1.9 copy.196
  118.6 0.4 fusion.7
  119.0 1.3 bitcast_convert_fusion
  120.6 61.6 %all-reduce.3.cloned.1.call-done = bf16[384,1024]{1,0:T(8,128)(2,1)} async-done(((bf16[384,1024]{1,0:T(8,128)(2,1)}), bf16[384,1024]{1,0:T(8,128)(2,1)}) %all-reduce.3.cloned.1.call-update) | async-done | bytes 786448 | tf_op jit(solution)/shard_map/psum | solution.py:101
  182.2 1.5 fusion.1
  183.7 0.4 multiply_reduce_fusion.1
  184.5 4.8 %convolution_convert_fusion = bf16[384,1024]{1,0:T(8,128)(2,1)} fusion(bf16[512,1024]{1,0:T(8,128)(2,1)S(1)} %copy-done, bf16[384,1024]{1,0:T(8,128)(2,1)S(1)} %multiply_convert_fusion.1, bf16[1024,512]{1,0:T(8,128)(2,1)} %param.17), kind=kOutput, calls=%fused_computation.20 | convolution fusion | flops 818479104 | bytes 3670016 | tf_op jit(solution)/shard_map/dot_general | solution.py:107
  189.4 66.1 %all-reduce.5.cloned.1.call-done = bf16[384,1024]{1,0:T(8,128)(2,1)} async-done(((bf16[384,1024]{1,0:T(8,128)(2,1)}), bf16[384,1024]{1,0:T(8,128)(2,1)}) %all-reduce.5.cloned.1.call-update) | async-done | bytes 786448 | tf_op jit(solution)/shard_map/psum | solution.py:106
  255.5 1.5 fusion.3
  257.5 0.6 multiply_reduce_fusion.2
  258.0 0.7 multiply_convert_fusion.3
  259.0 44.2 %all-gather = s32[32,12,8]{1,2,0:T(8,128)S(1)} all-gather(s32[1,12,8]{1,2,0:T(8,128)S(1)} %bitcast.95), channel_id=1, replica_groups=mesh['head'=8,'doc'=32] {'doc'}, dimensions={0}, use_global_device_ids=true | all-gather | bytes 12672 | tf_op jit(solution)/shard_map/all_gather | solution.py:126
  303.4 1.2 convert_reduce_fusion
  305.6 10.3 %gather_fusion.5 = bf16[192,256,128]{2,1,0:T(8,128)(2,1)} fusion(bf16[64,256,128]{2,1,0:T(8,128)(2,1)} %param.24, s32[1024]{0:T(1024)S(1)} %pad_clamp_fusion.1), kind=kCustom, calls=%fused_computation.5 | custom fusion | bytes 25166592 | tf_op jit(solution)/shard_map/gather | solution.py:32
  315.8 1.5 gather_fusion.3
  317.7 21.3 %all-gather.6.cloned.1.call-done = bf16[12288,128]{0,1:T(8,128)(2,1)} async-done(((bf16[384,128]{0,1:T(8,128)(2,1)}), bf16[12288,128]{0,1:T(8,128)(2,1)}) %all-gather.6.cloned.1.call-update) | async-done | bytes 3145744 | tf_op jit(solution)/shard_map/all_gather | solution.py:125
  339.0 4.7 %copy.206 = bf16[12288,128]{1,0:T(8,128)(2,1)} copy(bf16[12288,128]{0,1:T(8,128)(2,1)} %all-gather.6.cloned.1.call-done) | data formatting | bytes 6291456 | tf_op jit(solution)/shard_map/all_gather | solution.py:125
  343.8 3.7 gather_fusion.4
  347.5 9.2 %select_reduce_fusion = f32[192,32]{1,0:T(8,128)S(1)} fusion(pred[192,256]{1,0:T(8,128)(4,1)S(1)} %iota_compare_fusion, bf16[192,32,128]{2,1,0:T(8,128)(2,1)S(1)} %gather_fusion.4, bf16[192,256,128]{2,1,0:T(8,128)(2,1)} %gather_fusion.5), kind=kOutput, calls=%fused_computation.7 | convolution fusion | flops 405792768 | bytes 14229504 | tf_op jit(solution)/shard_map/sqe,sje->sqj/dot_general | solution.py:34
  356.9 0.7 copy.210
  357.6 9.0 %all-to-all-start = ((f32[32,1,6]{2,1,0:T(1,128)}), f32[32,1,6]{2,1,0:T(1,128)S(1)}, u32[]{:S(2)}, u32[]{:S(2)}) async-start(f32[32,1,6]{2,1,0:T(1,128)} %copy.210), calls=%async_computation | async-start | bytes 32768 | tf_op jit(solution)/shard_map/all_to_all | solution.py:144
  366.7 0.8 copy.213
  367.5 9.0 %all-to-all-done = f32[32,1,6]{2,1,0:T(1,128)S(1)} async-done(((f32[32,1,6]{2,1,0:T(1,128)}), f32[32,1,6]{2,1,0:T(1,128)S(1)}, u32[]{:S(2)}, u32[]{:S(2)}) %all-to-all-start) | async-done | bytes 800 | tf_op jit(solution)/shard_map/all_to_all | solution.py:144
  376.5 0.5 broadcast.589
  377.0 0.7 reduce.3
  377.8 1.3 gather_fusion.6
  379.1 0.7 copy.214
  (94 shorter events, 5.9 us)
Async XLA Ops:
  7.2 177.3 %copy-start = (bf16[512,1024]{1,0:T(8,128)(2,1)S(1)}, bf16[512,1024]{1,0:T(8,128)(2,1)}, u32[]{:S(2)}) copy-start(bf16[512,1024]{1,0:T(8,128)(2,1)} %param.18) | copy-start | bytes 3145732
  7.2 2.5 copy-start.6
  7.2 84.3 %all-gather.4.cloned.1.call-start = ((), (), s32[]{:S(2)}) async-start(), calls=%async_computation.1 | async-start | bytes 2162688 | tf_op jit(solution)/shard_map/all_gather | solution.py:63
  7.9 174.3 %all-reduce.3.cloned.1.call-start = ((), (), s32[]{:S(2)}) async-start(), calls=%async_computation.2 | async-start | bytes 1572864 | tf_op jit(solution)/shard_map/psum | solution.py:101
  30.6 2.9 copy-start.2
  55.9 8.7 %copy-start.15 = (s32[12]{0:T(128)S(1)}, s32[12]{0:T(128)}, u32[]{:S(2)}) copy-start(s32[12]{0:T(128)} %param.26) | copy-start | bytes 148
  115.6 1.9 copy-start.5
  117.5 1.0 copy-start.8
  117.5 1.1 copy-start.9
  117.8 1.2 copy-start.10
  120.4 63.8 %copy-start.12 = (f32[1024]{0:T(1024)S(1)}, f32[1024]{0:T(1024)}, u32[]{:S(2)}) copy-start(f32[1024]{0:T(1024)} %param.19) | copy-start | bytes 12292
  120.4 135.2 %all-reduce.5.cloned.1.call-start = ((), (), s32[]{:S(2)}) async-start(), calls=%async_computation.3 | async-start | bytes 1572864 | tf_op jit(solution)/shard_map/psum | solution.py:106
  182.2 1.5 copy-start.3
  189.4 68.1 %copy-start.13 = (bf16[1024,128]{1,0:T(8,128)(2,1)S(1)}, bf16[1024,128]{1,0:T(8,128)(2,1)}, u32[]{:S(2)}) copy-start(bf16[1024,128]{1,0:T(8,128)(2,1)} %param.23) | copy-start | bytes 786436
  189.4 68.1 %copy-start.14 = (f32[1024]{0:T(1024)S(1)}, f32[1024]{0:T(1024)}, u32[]{:S(2)}) copy-start(f32[1024]{0:T(1024)} %param.20) | copy-start | bytes 12292
  189.4 149.7 %all-gather.6.cloned.1.call-start = ((), (), s32[]{:S(2)}) async-start(), calls=%async_computation.4 | async-start | bytes 3244032 | tf_op jit(solution)/shard_map/all_gather | solution.py:125
  255.5 1.5 copy-start.4
  257.4 1.3 copy-start.11
  305.5 10.3 %copy-start.1 = (s32[64]{0:T(128)S(1)}, s32[64]{0:T(128)}, u32[]{:S(2)}) copy-start(s32[64]{0:T(128)} %param.25) | copy-start | bytes 772
  347.5 19.2 %copy-start.7 = (bf16[384,128]{0,1:T(8,128)(2,1)S(1)}, bf16[384,128]{0,1:T(8,128)(2,1)}, u32[]{:S(2)}) copy-start(bf16[384,128]{0,1:T(8,128)(2,1)} %multiply_convert_fusion.3) | copy-start | bytes 294916
  357.6 18.8 %all-to-all-start = ((f32[32,1,6]{2,1,0:T(1,128)}), f32[32,1,6]{2,1,0:T(1,128)S(1)}, u32[]{:S(2)}, u32[]{:S(2)}) async-start(f32[32,1,6]{2,1,0:T(1,128)} %copy.210), calls=%async_computation | async-start | bytes 32768 | tf_op jit(solution)/shard_map/all_to_all | solution.py:144
Sparse Core Ops, SparseCore 0:
  10.6 80.8 all-gather.3
  120.5 61.6 all-reduce.2
  189.5 65.9 all-reduce.4
  258.9 80.1 all-gather.5
where the time goes:
time: 387 us; the launch traced here: 386 us
  waiting for transfers between devices  185 us (48%)
  local copies, waits for them, and re-layouts  103 us (27%)
  blocking collectives  44.2 us (11%)
  matrix products  22.4 us (6%)
  between operations  14.2 us (4%)
  starting transfers between devices  9.37 us (2%)
  other arithmetic  8.49 us (2%)
    psum x1, waiting for transfers between devices, body(): lax.psum(jnp.dot(inner, w_down, preferred_element_type=jnp.float32).astyp...  66.1 us
    psum x1, waiting for transfers between devices, body(): lax.psum(attn_part.astype(jnp.bfloat16), 'head').astype(jnp.float32)  61.6 us
    all_gather x1, blocking collectives, body(): lax.all_gather(candidates, 'doc', axis=0, tiled=True)  44.2 us
    all_gather x1, waiting for transfers between devices, body(): gathered = lax.all_gather(prompt_cache, 'doc', axis=1, tiled=True)  25.8 us
    gather x2, local copies, waits for them, and re-layouts, body(): rel_k_rows = rel_both[1][:, index_one]  24.3 us
    gather x2, local copies, waits for them, and re-layouts, body(): rel_q_rows = rel_both[0][:, index_two]  23.2 us
    all_gather x1, waiting for transfers between devices, body(): lax.all_gather(query_vectors, 'doc', axis=0, tiled=True)  21.3 us
    reshape x2, local copies, waits for them, and re-layouts, body(): cache_all = gathered.reshape(2, groups_all, PLEN, heads_loc, HD)  13.7 us
  transfers between devices with their start and end apart: 5, of which 5 were waited for; matrix products, arithmetic and copies ran while one was open for 19% of the time, Pallas kernels for 0%

commit v1 on v0

--- a/solution.py
+++ b/solution.py
@@ -98,7 +98,9 @@
     attn_part = jnp.einsum(
         "hrqd,hde->rqe", attended, out_split, preferred_element_type=jnp.float32
     ).reshape(rows_dev, w_out.shape[1])
-    attn_total = lax.psum(attn_part.astype(jnp.bfloat16), "head").astype(jnp.float32)
+    attn_total = jnp.sum(lax.all_gather(attn_part.astype(jnp.bfloat16), "head"), axis=0).astype(
+        jnp.float32
+    )
     hidden_one = layer_norm(tokens.astype(jnp.float32) + attn_total, gain_one).astype(jnp.bfloat16)
     inner = jax.nn.gelu(
         jnp.dot(hidden_one, w_up, preferred_element_type=jnp.float32), approximate=False

time: 387 us -> 366 us (0.946)
  waiting for transfers between devices: 185 us -> 163 us
  local copies, waits for them, and re-layouts: 103 us -> 98.9 us
    psum x1 -> x0, waiting for transfers between devices: 61.6 us -> none  [body(): lax.psum(attn_part.astype(jnp.bfloat16), 'head').astype(jnp.float32)]
    all_gather x0 -> x1, waiting for transfers between devices: none -> 39.6 us  [body(): lax.all_gather(attn_part.astype(jnp.bfloat16), 'head')]
    reduce_sum x0 -> x1, other arithmetic: none -> 4.3 us  [body(): jnp.sum(lax.all_gather(attn_part.astype(jnp.bfloat16), 'head'), axis=0)]
  transfers between devices with their start and end apart: 5 -> 5, of which waited for: 5 -> 5; matrix products, arithmetic and copies ran while one was open for 19% -> 20% of each run, Pallas kernels for 0% -> 0%
where the time goes in v1:
time: 366 us; the launch traced here: 365 us
  waiting for transfers between devices  163 us (45%)
  local copies, waits for them, and re-layouts  98.9 us (27%)
  blocking collectives  44.3 us (12%)
  matrix products  23.7 us (6%)
  between operations  14.3 us (4%)
  other arithmetic  11.6 us (3%)
  starting transfers between devices  9.38 us (3%)
    psum x1, waiting for transfers between devices, body(): lax.psum(jnp.dot(inner, w_down, preferred_element_type=jnp.float32).astyp...  65.6 us
    all_gather x1, blocking collectives, body(): lax.all_gather(candidates, 'doc', axis=0, tiled=True)  44.3 us
    all_gather x1, waiting for transfers between devices, body(): lax.all_gather(attn_part.astype(jnp.bfloat16), 'head')  39.6 us
    all_gather x1, waiting for transfers between devices, body(): gathered = lax.all_gather(prompt_cache, 'doc', axis=1, tiled=True)  27 us
    gather x2, local copies, waits for them, and re-layouts, body(): rel_k_rows = rel_both[1][:, index_one]  25 us
    gather x2, local copies, waits for them, and re-layouts, body(): rel_q_rows = rel_both[0][:, index_two]  23.2 us
    all_gather x1, waiting for transfers between devices, body(): lax.all_gather(query_vectors, 'doc', axis=0, tiled=True)  21.1 us
    reshape x2, local copies, waits for them, and re-layouts, body(): cache_all = gathered.reshape(2, groups_all, PLEN, heads_loc, HD)  13.7 us
  transfers between devices with their start and end apart: 5, of which 5 were waited for; matrix products, arithmetic and copies ran while one was open for 20% of the time, Pallas kernels for 0%

profile of v1, /device:TPU:8, one launch (start us, length us, event | category | flops | bytes accessed | tf_op | source)
XLA Modules:
  0.0 365.3 jit_solution(2498960714608404057)
XLA Ops:
  7.2 0.7 all-gather.6.cloned.1.call-update
  8.2 1.4 copy.182
  9.7 0.5 fusion.9
  10.3 20.3 %gather_fusion.2 = bf16[3072,2,64]{2,1,0:T(2,128)(2,1)} fusion(bf16[2,512,64]{2,0,1:T(2,128)(2,1)S(1)} %copy.193, s32[3072]{0:T(1024)S(1)} %broadcast_clamp_fusion), kind=kCustom, calls=%fused_computation.2 | custom fusion | bytes 1585152 | tf_op jit(solution)/shard_map/gather | solution.py:85
  30.6 2.9 copy.194
  33.5 0.6 fusion.8
  34.4 0.9 copy.188
  35.6 20.3 %gather_fusion.1 = bf16[3072,2,64]{2,1,0:T(2,128)(2,1)} fusion(bf16[2,512,64]{2,0,1:T(2,128)(2,1)S(1)} %copy.189, s32[3072]{0:T(1024)S(1)} %broadcast_clamp_fusion.1), kind=kCustom, calls=%fused_computation.1 | custom fusion | bytes 1585152 | tf_op jit(solution)/shard_map/gather | solution.py:84
  55.9 4.7 %copy.190 = bf16[32,96,2,64]{1,3,0,2:T(8,128)(2,1)} copy(bf16[32,96,2,64]{3,2,1,0:T(2,128)(2,1)} %bitcast.85) | data formatting | bytes 1572864 | tf_op jit(solution)/shard_map/gather | solution.py:84
  61.0 1.0 copy.198
  62.0 2.5 fusion.11
  64.5 27.0 %all-gather.6.cloned.1.call-done = bf16[2,4096,128]{2,1,0:T(8,128)(2,1)} async-done(((bf16[2,128,128]{2,1,0:T(8,128)(2,1)}), bf16[2,4096,128]{2,1,0:T(8,128)(2,1)}) %all-gather.6.cloned.1.call-update) | async-done | bytes 2097168 | tf_op jit(solution)/shard_map/all_gather | solution.py:63
  91.5 8.2 %reshape.600 = bf16[2,64,64,2,64]{4,3,2,1,0:T(2,128)(2,1)} reshape(bf16[2,4096,128]{2,1,0:T(8,128)(2,1)} %all-gather.6.cloned.1.call-done) | data formatting | bytes 4194304 | tf_op jit(solution)/shard_map/reshape | solution.py:76
  99.7 5.4 %copy.186 = bf16[2,64,64,2,64]{4,2,3,1,0:T(8,128)(2,1)} copy(bf16[2,64,64,2,64]{4,3,2,1,0:T(2,128)(2,1)} %reshape.600) | data formatting | bytes 4194304 | tf_op jit(solution)/shard_map/reshape | solution.py:76
  105.2 2.9 gather_fusion
  108.1 0.4 copy.187
  108.5 0.8 slice_bitcast_fusion.1
  109.8 0.6 copy.195
  110.4 3.5 fusion.107
  113.9 1.9 copy.196
  116.9 0.4 fusion.7
  117.4 1.3 bitcast_convert_fusion
  118.9 39.6 %all-gather.10.cloned.1.call-done = bf16[3072,1024]{1,0:T(8,128)(2,1)} async-done(((bf16[384,1024]{1,0:T(8,128)(2,1)}), bf16[3072,1024]{1,0:T(8,128)(2,1)}) %all-gather.10.cloned.1.call-update) | async-done | bytes 6291472 | tf_op jit(solution)/shard_map/all_gather | solution.py:101
  158.6 4.3 %reduce_sum.118 = bf16[384,1024]{1,0:T(8,128)(2,1)S(1)} reduce(bf16[8,384,1024]{2,1,0:T(8,128)(2,1)} %bitcast.84, bf16[]{:T(256)} %constant.57.clone.1), dimensions={0}, to_apply=%region_2.0 | reduce | flops 2752512 | bytes 7077890 | tf_op jit(solution)/shard_map/reduce_sum | solution.py:101
  163.2 0.4 multiply_reduce_fusion.1
  163.6 0.4 multiply_convert_fusion.1
  164.0 4.8 %convolution_convert_fusion = bf16[384,1024]{1,0:T(8,128)(2,1)} fusion(bf16[512,1024]{1,0:T(8,128)(2,1)S(1)} %copy-done, bf16[384,1024]{1,0:T(8,128)(2,1)S(1)} %multiply_convert_fusion.1, bf16[1024,512]{1,0:T(8,128)(2,1)} %param.17), kind=kOutput, calls=%fused_computation.20 | convolution fusion | flops 818479104 | bytes 3670016 | tf_op jit(solution)/shard_map/dot_general | solution.py:109
  168.9 65.6 %all-reduce.2.cloned.1.call-done = bf16[384,1024]{1,0:T(8,128)(2,1)} async-done(((bf16[384,1024]{1,0:T(8,128)(2,1)}), bf16[384,1024]{1,0:T(8,128)(2,1)}) %all-reduce.2.cloned.1.call-update) | async-done | bytes 786448 | tf_op jit(solution)/shard_map/psum | solution.py:108
  234.5 1.5 fusion.3
  236.0 0.4 multiply_reduce_fusion
  236.4 0.6 multiply_reduce_fusion.2
  237.0 0.7 multiply_convert_fusion.3
  238.0 44.3 %all-gather.1 = s32[32,12,8]{1,2,0:T(8,128)S(1)} all-gather(s32[1,12,8]{1,2,0:T(8,128)S(1)} %bitcast.97), channel_id=1, replica_groups=mesh['head'=8,'doc'=32] {'doc'}, dimensions={0}, use_global_device_ids=true | all-gather | bytes 12672 | tf_op jit(solution)/shard_map/all_gather | solution.py:128
  282.6 1.2 convert_reduce_fusion
  284.7 10.3 %gather_fusion.5 = bf16[192,256,128]{2,1,0:T(8,128)(2,1)} fusion(bf16[64,256,128]{2,1,0:T(8,128)(2,1)} %param.24, s32[1024]{0:T(1024)S(1)} %pad_clamp_fusion.1), kind=kCustom, calls=%fused_computation.5 | custom fusion | bytes 25166592 | tf_op jit(solution)/shard_map/gather | solution.py:32
  295.0 1.5 gather_fusion.3
  296.8 21.1 %all-gather.8.cloned.1.call-done = bf16[12288,128]{0,1:T(8,128)(2,1)} async-done(((bf16[384,128]{0,1:T(8,128)(2,1)}), bf16[12288,128]{0,1:T(8,128)(2,1)}) %all-gather.8.cloned.1.call-update) | async-done | bytes 3145744 | tf_op jit(solution)/shard_map/all_gather | solution.py:127
  317.9 4.7 %copy.206 = bf16[12288,128]{1,0:T(8,128)(2,1)} copy(bf16[12288,128]{0,1:T(8,128)(2,1)} %all-gather.8.cloned.1.call-done) | data formatting | bytes 6291456 | tf_op jit(solution)/shard_map/all_gather | solution.py:127
  322.7 3.7 %gather_fusion.4 = bf16[192,32,128]{2,1,0:T(8,128)(2,1)S(1)} fusion(bf16[32,12,32,128]{3,2,1,0:T(8,128)(2,1)} %bitcast.83, s32[192]{0:T(256)S(1)} %reshape.565), kind=kCustom, calls=%fused_computation.4 | custom fusion | bytes 3147264 | tf_op jit(solution)/shard_map/gather | solution.py:144
  326.4 9.2 %select_reduce_fusion = f32[192,32]{1,0:T(8,128)S(1)} fusion(pred[192,256]{1,0:T(8,128)(4,1)S(1)} %iota_compare_fusion, bf16[192,32,128]{2,1,0:T(8,128)(2,1)S(1)} %gather_fusion.4, bf16[192,256,128]{2,1,0:T(8,128)(2,1)} %gather_fusion.5), kind=kOutput, calls=%fused_computation.7 | convolution fusion | flops 405792768 | bytes 14229504 | tf_op jit(solution)/shard_map/sqe,sje->sqj/dot_general | solution.py:34
  335.9 0.7 copy.210
  336.6 9.0 %all-to-all-start = ((f32[32,1,6]{2,1,0:T(1,128)}), f32[32,1,6]{2,1,0:T(1,128)S(1)}, u32[]{:S(2)}, u32[]{:S(2)}) async-start(f32[32,1,6]{2,1,0:T(1,128)} %copy.210), calls=%async_computation | async-start | bytes 32768 | tf_op jit(solution)/shard_map/all_to_all | solution.py:146
  345.6 0.8 copy.213
  346.4 9.0 %all-to-all-done = f32[32,1,6]{2,1,0:T(1,128)S(1)} async-done(((f32[32,1,6]{2,1,0:T(1,128)}), f32[32,1,6]{2,1,0:T(1,128)S(1)}, u32[]{:S(2)}, u32[]{:S(2)}) %all-to-all-start) | async-done | bytes 800 | tf_op jit(solution)/shard_map/all_to_all | solution.py:146
  355.4 0.5 broadcast.589
  355.9 0.7 reduce.4
  356.7 1.3 gather_fusion.6
  358.0 0.7 copy.214
  (101 shorter events, 5.8 us)
Async XLA Ops:
  7.2 156.8 %copy-start = (bf16[512,1024]{1,0:T(8,128)(2,1)S(1)}, bf16[512,1024]{1,0:T(8,128)(2,1)}, u32[]{:S(2)}) copy-start(bf16[512,1024]{1,0:T(8,128)(2,1)} %param.18) | copy-start | bytes 3145732
  7.2 2.5 copy-start.9
  7.2 84.3 %all-gather.6.cloned.1.call-start = ((), (), s32[]{:S(2)}) async-start(), calls=%async_computation.1 | async-start | bytes 2162688 | tf_op jit(solution)/shard_map/all_gather | solution.py:63
  7.9 150.6 %all-gather.10.cloned.1.call-start = ((), (), s32[]{:S(2)}) async-start(), calls=%async_computation.4 | async-start | bytes 7077888 | tf_op jit(solution)/shard_map/all_gather | solution.py:101
  30.6 2.9 copy-start.3
  55.9 6.1 %copy-start.18 = (s32[12]{0:T(128)S(1)}, s32[12]{0:T(128)}, u32[]{:S(2)}) copy-start(s32[12]{0:T(128)} %param.26) | copy-start | bytes 148
  60.8 38.9 %copy-start.5 = (bf16[1,2,384,64]{3,2,1,0:T(8,128)(2,1)}, bf16[1,2,384,64]{3,2,1,0:T(8,128)(2,1)S(1)}, u32[]{:S(2)}) copy-start(bf16[1,2,384,64]{3,2,1,0:T(8,128)(2,1)S(1)} %copy.183) | copy-start | bytes 294916
  108.5 1.1 copy-start.8
  113.9 1.9 copy-start.6
  113.9 1.9 copy-start.7
  115.8 1.0 copy-start.11
  115.8 1.1 copy-start.12
  116.2 1.2 copy-start.13
  118.7 115.8 %all-reduce.2.cloned.1.call-start = ((), (), s32[]{:S(2)}) async-start(), calls=%async_computation.2 | async-start | bytes 1572864 | tf_op jit(solution)/shard_map/psum | solution.py:108
  162.9 0.7 copy-start.15
  168.8 67.6 %copy-start.16 = (bf16[1024,128]{1,0:T(8,128)(2,1)S(1)}, bf16[1024,128]{1,0:T(8,128)(2,1)}, u32[]{:S(2)}) copy-start(bf16[1024,128]{1,0:T(8,128)(2,1)} %param.23) | copy-start | bytes 786436
  168.8 67.6 %copy-start.17 = (f32[1024]{0:T(1024)S(1)}, f32[1024]{0:T(1024)}, u32[]{:S(2)}) copy-start(f32[1024]{0:T(1024)} %param.20) | copy-start | bytes 12292
  168.8 149.1 %all-gather.8.cloned.1.call-start = ((), (), s32[]{:S(2)}) async-start(), calls=%async_computation.3 | async-start | bytes 3244032 | tf_op jit(solution)/shard_map/all_gather | solution.py:127
  234.5 1.5 copy-start.4
  236.4 1.3 copy-start.14
  284.7 10.3 %copy-start.2 = (s32[64]{0:T(128)S(1)}, s32[64]{0:T(128)}, u32[]{:S(2)}) copy-start(s32[64]{0:T(128)} %param.25) | copy-start | bytes 772
  326.4 19.3 %copy-start.10 = (bf16[384,128]{0,1:T(8,128)(2,1)S(1)}, bf16[384,128]{0,1:T(8,128)(2,1)}, u32[]{:S(2)}) copy-start(bf16[384,128]{0,1:T(8,128)(2,1)} %multiply_convert_fusion.3) | copy-start | bytes 294916
  326.4 32.4 %copy-start.1 = (bf16[512,1024]{1,0:T(8,128)(2,1)S(1)}, bf16[512,1024]{1,0:T(8,128)(2,1)}, u32[]{:S(2)}) copy-start(bf16[512,1024]{1,0:T(8,128)(2,1)} %param.18) | copy-start | bytes 3145732
  336.6 18.8 %all-to-all-start = ((f32[32,1,6]{2,1,0:T(1,128)}), f32[32,1,6]{2,1,0:T(1,128)S(1)}, u32[]{:S(2)}, u32[]{:S(2)}) async-start(f32[32,1,6]{2,1,0:T(1,128)} %copy.210), calls=%async_computation | async-start | bytes 32768 | tf_op jit(solution)/shard_map/all_to_all | solution.py:146
Sparse Core Ops, SparseCore 0:
  10.6 80.8 all-gather.5
  118.8 39.7 all-gather.9
  168.9 65.5 all-reduce.1
  237.8 80.0 all-gather.7
